TPU v7x, 32 devices: a whole 2x2x4 slice. The times are simulated.
32 devices in a mesh: seq: 16 (over z, y, core), chan: 2 (over x).
Axes of the slice: x: 2, y: 2, z: 4, core: 2. Of those that a mesh axis runs over, the one named last changes fastest.
Arguments:
- inputs: bfloat16 [512, 512, 512], P('chan', 'seq'), may hold values from -6 to 6
- gate_in: bfloat16 [512, 512, 512], P('chan', 'seq'), may hold values from -6 to 6
- gate_out: bfloat16 [512, 512, 512], P('seq', 'chan'), may hold values from -6 to 6
- cotangent: bfloat16 [512, 512, 512], P('seq', 'chan'), may hold values from -6 to 6
- mix_one: bfloat16 [512, 512, 512], P('seq', 'chan'), may hold values from -6 to 6
- second_mixing_blocks: bfloat16 [512, 512, 512], P('seq', 'chan'), may hold values from -6 to 6
Outputs:
- grad_input: bfloat16 [512, 512, 512], P('chan', 'seq')
- grad_gate_out: bfloat16 [512, 512, 512], P('seq', 'chan')
- grad_mix_one: bfloat16 [512, 512, 512], P('seq', 'chan')
- grad_mix_two: bfloat16 [512, 512, 512], P('seq', 'chan')
All inputs are finite; a program needn't handle non-finite values.
Results may differ from a plain program's by a relative error of at most 0.0095.
Values may be sent and summed in bfloat16 or wider, within the bound.
A program may use at most 256 MiB of HBM per device.

v0:
```python
import math
import jax
import jax.numpy as jnp
from jax import lax
from jax.sharding import PartitionSpec as P


def shards(inputs, gate_in, gate_out, cotangent, mix_one, second_mixing_blocks):
    chan_count = lax.axis_size("chan")
    first_scale = 1.0 / math.sqrt(mix_one.shape[2])
    scale_two = 1.0 / math.sqrt(second_mixing_blocks.shape[2])
    gated = (inputs.astype(jnp.float32) * gate_in.astype(jnp.float32)).astype(jnp.bfloat16)
    grad_second = (cotangent.astype(jnp.float32) * gate_out.astype(jnp.float32)).astype(
        jnp.bfloat16
    )
    gated_all = lax.all_gather(gated, "chan", axis=0, tiled=True)
    full_one, full_two = (
        lax.all_gather(mix_one, "chan", axis=1, tiled=True),
        lax.all_gather(second_mixing_blocks, "chan", axis=1, tiled=True),
    )
    first = (
        jnp.einsum("roi,dri->odr", full_one, gated, preferred_element_type=jnp.float32)
        * first_scale
    ).astype(jnp.bfloat16)
    first_cols = lax.all_to_all(first, "seq", split_axis=0, concat_axis=2, tiled=True)
    first_all = lax.all_gather(first_cols, "chan", axis=1, tiled=True)
    second = (
        jnp.einsum("coi,cdi->cdo", full_two, first_cols, preferred_element_type=jnp.float32)
        * scale_two
    ).astype(jnp.bfloat16)
    grad_gate_out = (cotangent.astype(jnp.float32) * second.astype(jnp.float32)).astype(
        jnp.bfloat16
    )
    grad_first_cols = (
        jnp.einsum("coi,cdo->cdi", full_two, grad_second, preferred_element_type=jnp.float32)
        * scale_two
    ).astype(jnp.bfloat16)
    grad_second_rows = lax.all_to_all(grad_second, "chan", split_axis=2, concat_axis=1, tiled=True)
    grad_mix_two = (
        jnp.einsum("cdo,cdi->coi", grad_second_rows, first_all, preferred_element_type=jnp.float32)
        * scale_two
    ).astype(jnp.bfloat16)
    grad_first = lax.all_to_all(grad_first_cols, "seq", split_axis=2, concat_axis=0, tiled=True)
    grad_part = lax.all_to_all(grad_first, "chan", split_axis=0, concat_axis=1, tiled=True)
    grad_mix_one = (
        jnp.einsum("odr,dri->roi", grad_part, gated_all, preferred_element_type=jnp.float32)
        * first_scale
    ).astype(jnp.bfloat16)
    rows_here, columns, _ = full_one.shape
    group_weight = full_one.reshape(rows_here, chan_count, columns // chan_count, columns)
    group_grad = grad_first.reshape(
        chan_count, columns // chan_count, grad_first.shape[1], rows_here
    )
    summand_terms = (
        jnp.einsum("rgoi,godr->gdri", group_weight, group_grad, preferred_element_type=jnp.float32)
        * first_scale
    ).astype(jnp.bfloat16)
    grad_gated = jnp.sum(summand_terms.astype(jnp.float32), axis=0).astype(jnp.bfloat16)
    grad_input = (grad_gated.astype(jnp.float32) * gate_in.astype(jnp.float32)).astype(jnp.bfloat16)
    return (grad_input, grad_gate_out, grad_mix_one, grad_mix_two)


def solution(mesh):
    return jax.shard_map(
        shards,
        mesh=mesh,
        in_specs=(
            P("chan", "seq", None),
            P("chan", "seq", None),
            P("seq", "chan", None),
            P("seq", "chan", None),
            P("seq", "chan", None),
            P("seq", "chan", None),
        ),
        out_specs=(
            P("chan", "seq", None),
            P("seq", "chan", None),
            P("seq", "chan", None),
            P("seq", "chan", None),
        ),
        check_vma=False,
    )
```

profile of v0, /device:TPU:0, one launch (start us, length us, event | category | flops | bytes accessed | tf_op | source)
XLA Modules:
  0.0 1185.1 jit_solution(13639298940770544008)
XLA Ops:
  7.2 0.0 all-gather.5.cloned.1.call-start
  7.2 0.7 all-gather.5.cloned.1.call-update
  7.9 0.0 all-gather.7.cloned.1.call-start
  7.9 0.7 all-gather.7.cloned.1.call-update
  8.6 0.0 all-gather.9.cloned.1.call-start
  8.7 9.9 fusion
  18.6 192.5 %all-gather.5.cloned.1.call-done = bf16[32,512,512]{2,1,0:T(8,128)(2,1)} async-done(((bf16[32,256,512]{2,1,0:T(8,128)(2,1)}), bf16[32,512,512]{2,1,0:T(8,128)(2,1)}) %all-gather.5.cloned.1.call-update) | async-done | bytes 16777232 | tf_op jit(solution)/shard_map/all_gather | solution.py:19
  211.1 15.1 %multiply_convert_fusion.5 = bf16[32,256,512]{2,1,0:T(8,128)(2,1)} fusion(bf16[32,256,512]{2,1,0:T(8,128)(2,1)} %fusion, bf16[32,512,512]{2,1,0:T(8,128)(2,1)} %all-gather.5.cloned.1.call-done), kind=kOutput, calls=%fused_computation.14 | convolution fusion | flops 4303355904 | bytes 33554432 | tf_op jit(solution)/shard_map/coi,cdo->cdi/dot_general | solution.py:35
  226.2 15.2 %copy.29 = bf16[32,256,512]{1,0,2:T(8,128)(2,1)} copy(bf16[32,256,512]{2,1,0:T(8,128)(2,1)} %multiply_convert_fusion.5) | data formatting | bytes 16777216 | tf_op jit(solution)/shard_map/convert_element_type | solution.py:37
  241.4 188.0 %all_to_all.72 = bf16[32,256,512]{1,0,2:T(8,128)(2,1)} all-to-all(bf16[32,256,512]{1,0,2:T(8,128)(2,1)} %copy.29), channel_id=1, replica_groups=mesh['seq'=16,'chan'=2] {'seq'}, dimensions={2} | all-to-all | bytes 16777216 | tf_op jit(solution)/shard_map/all_to_all | solution.py:43
  429.4 12.5 %copy.31 = bf16[16,32,256,32]{2,3,1,0:T(8,128)(2,1)} copy(bf16[16,32,256,32]{2,1,3,0:T(8,128)(2,1)} %bitcast.42) | data formatting | bytes 16777216 | tf_op jit(solution)/shard_map/all_to_all | solution.py:43
  441.8 26.4 %fusion.7 = bf16[32,256,512]{2,1,0:T(8,128)(2,1)} fusion(bf16[32,2,256,512]{3,2,1,0:T(8,128)(2,1)} %bitcast.45, bf16[2,256,256,32]{2,3,1,0:T(8,128)(2,1)} %bitcast.39), kind=kOutput, calls=%fused_computation.18 | convolution fusion | flops 4315938816 | bytes 33554432 | tf_op jit(solution)/shard_map/rgoi,godr->gdri/dot_general | solution.py:55
  468.2 18.1 %fusion.3 = (bf16[256,32,512]{2,0,1:T(8,128)(2,1)}, bf16[256,32,512]{2,0,1:T(8,128)(2,1)}) fusion(bf16[256,32,512]{2,1,0:T(8,128)(2,1)} %param.6, bf16[256,32,512]{2,1,0:T(8,128)(2,1)} %param.7, bf16[32,256,512]{2,1,0:T(8,128)(2,1)} %fusion.7), kind=kLoop, calls=%fused_computation.8 | loop fusion | flops 29360128 | bytes 41943040 | tf_op jit(solution)/shard_map/convert_element_type | solution.py:12
  486.4 0.0 all-gather.9.cloned.1.call-update
  486.4 0.0 all-gather.11.cloned.1.call-start
  486.5 16.1 %fusion.6 = bf16[512,256,32]{0,1,2:T(8,128)(2,1)} fusion(bf16[256,32,512]{2,0,1:T(8,128)(2,1)} %get-tuple-element.16, bf16[32,512,512]{2,1,0:T(8,128)(2,1)} %all-gather.7.cloned.1.call-done), kind=kOutput, calls=%fused_computation.17 | convolution fusion | flops 4303355904 | bytes 33554432 | tf_op jit(solution)/shard_map/roi,dri->odr/dot_general | solution.py:22
  502.6 15.2 %copy.36 = bf16[512,256,32]{1,2,0:T(8,128)(2,1)} copy(bf16[512,256,32]{0,1,2:T(8,128)(2,1)} %fusion.6) | data formatting | bytes 16777216 | tf_op jit(solution)/shard_map/convert_element_type | solution.py:24
  517.8 187.7 %all_to_all.73 = bf16[512,256,32]{1,2,0:T(8,128)(2,1)} all-to-all(bf16[512,256,32]{1,2,0:T(8,128)(2,1)} %copy.36), channel_id=1, replica_groups=mesh['seq'=16,'chan'=2] {'seq'}, dimensions={0} | all-to-all | bytes 16777216 | tf_op jit(solution)/shard_map/all_to_all | solution.py:25
  705.5 8.0 copy.37
  713.5 12.0 %copy.43 = bf16[32,256,512]{2,1,0:T(8,128)(2,1)} copy(bf16[32,256,512]{1,2,0:T(8,128)(2,1)} %bitcast.37) | data formatting | bytes 16777216 | tf_op jit(solution)/shard_map/all_to_all | solution.py:25
  725.5 15.3 %copy.41 = bf16[32,256,512]{1,0,2:T(8,128)(2,1)} copy(bf16[32,256,512]{2,1,0:T(8,128)(2,1)} %fusion) | data formatting | bytes 16777216 | tf_op jit(solution)/shard_map/convert_element_type | solution.py:13
  740.8 195.0 %all_to_all.74 = bf16[32,256,512]{1,0,2:T(8,128)(2,1)} all-to-all(bf16[32,256,512]{1,0,2:T(8,128)(2,1)} %copy.41), channel_id=1, replica_groups=mesh['seq'=16,'chan'=2] {'chan'}, dimensions={2} | all-to-all | bytes 16777216 | tf_op jit(solution)/shard_map/all_to_all | solution.py:38
  935.8 7.0 all-to-all-start.2
  942.8 16.7 %copy.60 = bf16[32,256,2,256]{1,2,3,0:T(2,128)(2,1)} copy(bf16[32,256,2,256]{1,0,3,2:T(8,128)(2,1)} %bitcast.41) | data formatting | bytes 16777216 | tf_op jit(solution)/shard_map/all_to_all | solution.py:38
  959.5 14.1 %all_to_all.67 = bf16[32,512,256]{1,2,0:T(8,128)(2,1)} reshape(bf16[32,2,256,256]{2,1,3,0:T(2,128)(2,1)} %bitcast.44) | data formatting | bytes 16777216 | tf_op jit(solution)/shard_map/all_to_all | solution.py:38
  973.6 11.5 copy.44
  985.1 119.2 %all-to-all-done.2 = bf16[512,256,32]{1,2,0:T(8,128)(2,1)} async-done(((bf16[512,256,32]{1,2,0:T(8,128)(2,1)}), bf16[512,256,32]{1,2,0:T(8,128)(2,1)}, u32[]{:S(2)}, u32[]{:S(2)}) %all-to-all-start.2) | async-done | bytes 8388640 | tf_op jit(solution)/shard_map/all_to_all | solution.py:44
  1104.3 16.5 %copy.40 = bf16[256,2,256,32]{2,1,0,3:T(2,128)(2,1)} copy(bf16[256,2,256,32]{2,3,0,1:T(8,128)(2,1)} %bitcast.14) | data formatting | bytes 16777216 | tf_op jit(solution)/shard_map/all_to_all | solution.py:44
  1120.8 14.1 %all_to_all.63 = bf16[256,512,32]{1,0,2:T(8,128)(2,1)} reshape(bf16[256,2,256,32]{2,1,0,3:T(2,128)(2,1)} %copy.40) | data formatting | bytes 16777216 | tf_op jit(solution)/shard_map/all_to_all | solution.py:44
  1134.8 15.6 %fusion.1 = bf16[32,256,512]{2,1,0:T(8,128)(2,1)} fusion(bf16[32,256,512]{2,1,0:T(8,128)(2,1)} %param.9, bf16[32,256,512]{1,2,0:T(8,128)(2,1)} %bitcast.38, bf16[32,512,512]{2,1,0:T(8,128)(2,1)} %all-gather.5.cloned.1.call-done), kind=kOutput, calls=%fused_computation.6 | convolution fusion | flops 4320133120 | bytes 41943040 | tf_op jit(solution)/shard_map/coi,cdi->cdo/dot_general | solution.py:28
  1150.5 14.0 %multiply_convert_fusion.2 = bf16[32,256,512]{2,1,0:T(8,128)(2,1)} fusion(bf16[256,512,32]{1,0,2:T(8,128)(2,1)} %all_to_all.63, bf16[512,32,512]{2,0,1:T(8,128)(2,1)} %all-gather.9.cloned.1.call-done), kind=kOutput, calls=%fused_computation.11 | convolution fusion | flops 4303355904 | bytes 33554432 | tf_op jit(solution)/shard_map/odr,dri->roi/dot_general | solution.py:46
  1164.5 13.8 %multiply_convert_fusion.1 = bf16[32,256,512]{2,1,0:T(8,128)(2,1)} fusion(bf16[32,512,256]{1,2,0:T(8,128)(2,1)} %all_to_all.67, bf16[32,512,512]{2,1,0:T(8,128)(2,1)} %all-gather.11.cloned.1.call-done), kind=kOutput, calls=%fused_computation.10 | convolution fusion | flops 4303355904 | bytes 33554432 | tf_op jit(solution)/shard_map/cdo,cdi->coi/dot_general | solution.py:40
  (4 shorter events, 0.0 us)
Async XLA Ops:
  7.2 204.0 %all-gather.5.cloned.1.call-start = ((), (), s32[]{:S(2)}) async-start(), calls=%async_computation.4 | async-start | bytes 25165824 | tf_op jit(solution)/shard_map/all_gather | solution.py:19
  7.9 433.9 %all-gather.7.cloned.1.call-start = ((), (), s32[]{:S(2)}) async-start(), calls=%async_computation.5 | async-start | bytes 25165824 | tf_op jit(solution)/shard_map/all_gather | solution.py:18
  8.6 1141.8 %all-gather.9.cloned.1.call-start = ((), (), s32[]{:S(2)}) async-start(), calls=%async_computation.6 | async-start | bytes 25165824 | tf_op jit(solution)/shard_map/all_gather | solution.py:16
  486.4 678.1 %all-gather.11.cloned.1.call-start = ((), (), s32[]{:S(2)}) async-start(), calls=%async_computation.7 | async-start | bytes 25165824 | tf_op jit(solution)/shard_map/all_gather | solution.py:26
  935.8 168.5 %all-to-all-start.2 = ((bf16[512,256,32]{1,2,0:T(8,128)(2,1)}), bf16[512,256,32]{1,2,0:T(8,128)(2,1)}, u32[]{:S(2)}, u32[]{:S(2)}) async-start(bf16[512,256,32]{1,2,0:T(8,128)(2,1)} %bitcast.40), calls=%async_computation.2 | async-start | bytes 16777216 | tf_op jit(solution)/shard_map/all_to_all | solution.py:44
Sparse Core Ops, SparseCore 0:
  9.5 201.5 all-gather.4
  212.7 198.8 all-gather.6
  486.5 198.9 all-gather.8
  725.7 357.3 all-gather.10
where the time goes:
time: 1190 us
  blocking collectives  571 us (48%)
  waiting for transfers between devices  313 us (26%)
  local copies, waits for them, and re-layouts  151 us (13%)
  matrix products  101 us (8%)
  other arithmetic  28 us (2%)
  between operations  14 us (1%)
    all_to_all x1, blocking collectives, shards(): lax.all_to_all(grad_second, 'chan', split_axis=2, concat_axis=1, tiled=True)  195 us
    all_gather x1, waiting for transfers between devices, shards(): lax.all_gather(second_mixing_blocks, 'chan', axis=1, tiled=True)  193 us
    all_to_all x1, blocking collectives, shards(): lax.all_to_all(grad_first_cols, 'seq', split_axis=2, concat_axis=0, tiled...  188 us
    all_to_all x1, blocking collectives, shards(): lax.all_to_all(first, 'seq', split_axis=0, concat_axis=2, tiled=True)  188 us
    all_to_all x1, waiting for transfers between devices, shards(): lax.all_to_all(grad_first, 'chan', split_axis=0, concat_axis=1, tiled=True)  119 us
    all_to_all x2, local copies, waits for them, and re-layouts, shards(): lax.all_to_all(grad_second, 'chan', split_axis=2, concat_axis=1, tiled=True)  30.8 us
    all_to_all x2, local copies, waits for them, and re-layouts, shards(): lax.all_to_all(grad_first, 'chan', split_axis=0, concat_axis=1, tiled=True)  30.6 us
    dot_general x1, matrix products, shards(): jnp.einsum('rgoi,godr->gdri', group_weight, group_grad, preferred_element...  26.4 us
  transfers between devices with their start and end apart: 5, of which 2 were waited for; matrix products, arithmetic and copies ran while one was open for 16% of the time, Pallas kernels for 0%

commit v1 on v0

--- a/solution.py
+++ b/solution.py
@@ -40,7 +40,9 @@
         jnp.einsum("cdo,cdi->coi", grad_second_rows, first_all, preferred_element_type=jnp.float32)
         * scale_two
     ).astype(jnp.bfloat16)
-    grad_first = lax.all_to_all(grad_first_cols, "seq", split_axis=2, concat_axis=0, tiled=True)
+    parts = jnp.split(grad_first_cols, lax.axis_size("seq"), axis=2)
+    received = lax.all_to_all(jnp.stack(parts), "seq", 0, 0)
+    grad_first = jnp.concatenate(received, axis=0)
     grad_part = lax.all_to_all(grad_first, "chan", split_axis=0, concat_axis=1, tiled=True)
     grad_mix_one = (
         jnp.einsum("odr,dri->roi", grad_part, gated_all, preferred_element_type=jnp.float32)

time: 1190 us -> 1240 us (1.042)
  blocking collectives: 571 us -> 418 us
  waiting for transfers between devices: 313 us -> 463 us
  local copies, waits for them, and re-layouts: 151 us -> 201 us
    all_to_all x1 -> x0, blocking collectives: 188 us -> none  [shards(): lax.all_to_all(grad_first_cols, 'seq', split_axis=2, concat_axis=0, tiled...]
    all_gather x1, waiting for transfers between devices: 0.01 us -> 104 us  [shards(): lax.all_gather(mix_one, 'chan', axis=1, tiled=True)]
    another operation x0 -> x18, local copies, waits for them, and re-layouts: none -> 53.1 us  [shards(): received = lax.all_to_all(jnp.stack(parts), 'seq', 0, 0)]
    all_to_all x0 -> x1, waiting for transfers between devices: none -> 45.8 us  [shards(): received = lax.all_to_all(jnp.stack(parts), 'seq', 0, 0)]
    all_to_all x1, blocking collectives: 188 us -> 223 us  [shards(): lax.all_to_all(first, 'seq', split_axis=0, concat_axis=2, tiled=True)]
    unnamed x1 -> x22, local copies, waits for them, and re-layouts: 11.5 us -> 36.4 us
    convert_element_type x1 -> x0, local copies, waits for them, and re-layouts: 15.2 us -> none  [shards(): grad_first_cols = (jnp.einsum('coi,cdo->cdi', full_two, grad_second, pref...]
    all_to_all x1 -> x0, local copies, waits for them, and re-layouts: 12.5 us -> none  [shards(): lax.all_to_all(grad_first_cols, 'seq', split_axis=2, concat_axis=0, tiled...]
  transfers between devices with their start and end apart: 5 -> 6, of which waited for: 2 -> 4; matrix products, arithmetic and copies ran while one was open for 16% -> 19% of each run, Pallas kernels for 0% -> 0%
where the time goes in v1:
time: 1240 us; the launch traced here: 1230 us
  waiting for transfers between devices  463 us (37%)
  blocking collectives  418 us (34%)
  local copies, waits for them, and re-layouts  201 us (16%)
  matrix products  94.2 us (8%)
  other arithmetic  28 us (2%)
  between operations  14.1 us (1%)
  starting transfers between devices  13.4 us (1%)
    all_to_all x1, blocking collectives, shards(): lax.all_to_all(first, 'seq', split_axis=0, concat_axis=2, tiled=True)  223 us
    all_to_all x1, blocking collectives, shards(): lax.all_to_all(grad_second, 'chan', split_axis=2, concat_axis=1, tiled=True)  195 us
    all_gather x1, waiting for transfers between devices, shards(): lax.all_gather(second_mixing_blocks, 'chan', axis=1, tiled=True)  193 us
    all_to_all x1, waiting for transfers between devices, shards(): lax.all_to_all(grad_first, 'chan', split_axis=0, concat_axis=1, tiled=True)  119 us
    all_gather x1, waiting for transfers between devices, shards(): lax.all_gather(mix_one, 'chan', axis=1, tiled=True)  104 us
    another operation x18, local copies, waits for them, and re-layouts, shards(): received = lax.all_to_all(jnp.stack(parts), 'seq', 0, 0)  53.1 us
    all_to_all x1, waiting for transfers between devices, shards(): received = lax.all_to_all(jnp.stack(parts), 'seq', 0, 0)  45.8 us
    unnamed x22, local copies, waits for them, and re-layouts  36.4 us
  transfers between devices with their start and end apart: 6, of which 4 were waited for; matrix products, arithmetic and copies ran while one was open for 19% of the time, Pallas kernels for 0%

profile of v1, /device:TPU:0, one launch (start us, length us, event | category | flops | bytes accessed | tf_op | source)
XLA Modules:
  0.0 1231.2 jit_solution(962697133572120252)
XLA Ops:
  8.6 9.9 fusion
  18.5 192.6 %all-gather.5.cloned.1.call-done = bf16[32,512,512]{2,1,0:T(8,128)(2,1)} async-done(((bf16[32,256,512]{2,1,0:T(8,128)(2,1)}), bf16[32,512,512]{2,1,0:T(8,128)(2,1)}) %all-gather.5.cloned.1.call-update) | async-done | bytes 16777232 | tf_op jit(solution)/shard_map/all_gather | solution.py:19
  211.1 11.8 multiply_convert_fusion.5
  222.9 16.3 %slice_bitcast_fusion = (bf16[1,32,256,32]{3,2,1,0:T(8,128)(2,1)}, bf16[1,32,256,32]{3,2,1,0:T(8,128)(2,1)}, bf16[1,32,256,32]{3,2,1,0:T(8,128)(2,1)}, bf16[1,32...) fusion(bf16[32,256,512]{2,1,0:T(8,128)(2,1)S(1)} %multiply_conv, ...), kind=kLoop, calls=%fused_computation.20 | loop fusion | bytes 16777216 | tf_op jit(solution)/shard_map/stack | solution.py:44
  243.5 2.6 copy.60
  250.2 2.7 copy.57
  252.9 2.6 copy.56
  255.5 2.6 copy.55
  276.3 2.6 copy.67
  278.9 2.6 copy.66
  301.0 5.8 all-to-all-start
  307.3 104.3 %all-gather.7.cloned.1.call-done = bf16[32,512,512]{2,1,0:T(8,128)(2,1)} async-done(((bf16[32,256,512]{2,1,0:T(8,128)(2,1)}), bf16[32,512,512]{2,1,0:T(8,128)(2,1)}) %all-gather.7.cloned.1.call-update) | async-done | bytes 16777232 | tf_op jit(solution)/shard_map/all_gather | solution.py:18
  411.5 45.8 %all-to-all-done = bf16[16,32,256,32]{2,3,1,0:T(8,128)(2,1)} async-done(((bf16[16,32,256,32]{2,3,1,0:T(8,128)(2,1)}), bf16[16,32,256,32]{2,3,1,0:T(8,128)(2,1)}, u32[]{:S(2)}, u32[]{:S(2)}) %all-to-all-start) | async-done | bytes 8388640 | tf_op jit(solution)/shard_map/all_to_all | solution.py:44
  457.3 25.9 %fusion.7 = bf16[32,256,512]{2,1,0:T(8,128)(2,1)} fusion(bf16[32,2,256,512]{3,2,1,0:T(8,128)(2,1)} %bitcast.71, bf16[2,256,256,32]{2,3,1,0:T(8,128)(2,1)} %bitcast.16), kind=kOutput, calls=%fused_computation.19 | convolution fusion | flops 4315938816 | bytes 33554432 | tf_op jit(solution)/shard_map/rgoi,godr->gdri/dot_general | solution.py:57
  483.2 18.1 %fusion.3 = (bf16[256,32,512]{2,0,1:T(8,128)(2,1)}, bf16[256,32,512]{2,0,1:T(8,128)(2,1)}) fusion(bf16[256,32,512]{2,1,0:T(8,128)(2,1)} %param.6, bf16[256,32,512]{2,1,0:T(8,128)(2,1)} %param.7, bf16[32,256,512]{2,1,0:T(8,128)(2,1)} %fusion.7), kind=kLoop, calls=%fused_computation.8 | loop fusion | flops 29360128 | bytes 41943040 | tf_op jit(solution)/shard_map/convert_element_type | solution.py:12
  501.4 13.1 %fusion.6 = bf16[512,256,32]{0,1,2:T(8,128)(2,1)} fusion(bf16[256,32,512]{2,0,1:T(8,128)(2,1)} %get-tuple-element.20, bf16[32,512,512]{2,1,0:T(8,128)(2,1)} %all-gather.7.cloned.1.call-done), kind=kOutput, calls=%fused_computation.18 | convolution fusion | flops 4303355904 | bytes 33554432 | tf_op jit(solution)/shard_map/roi,dri->odr/dot_general | solution.py:22
  514.5 14.6 %copy.75 = bf16[512,256,32]{1,2,0:T(8,128)(2,1)} copy(bf16[512,256,32]{0,1,2:T(8,128)(2,1)} %fusion.6) | data formatting | bytes 16777216 | tf_op jit(solution)/shard_map/convert_element_type | solution.py:24
  529.1 222.6 %all_to_all.59 = bf16[512,256,32]{1,2,0:T(8,128)(2,1)} all-to-all(bf16[512,256,32]{1,2,0:T(8,128)(2,1)} %copy.75), channel_id=1, replica_groups=mesh['seq'=16,'chan'=2] {'seq'}, dimensions={0} | all-to-all | bytes 16777216 | tf_op jit(solution)/shard_map/all_to_all | solution.py:25
  751.7 8.0 copy.76
  759.7 11.9 copy.81
  771.7 15.3 %copy.79 = bf16[32,256,512]{1,0,2:T(8,128)(2,1)} copy(bf16[32,256,512]{2,1,0:T(8,128)(2,1)} %fusion) | data formatting | bytes 16777216 | tf_op jit(solution)/shard_map/convert_element_type | solution.py:13
  787.0 195.0 %all_to_all.60 = bf16[32,256,512]{1,0,2:T(8,128)(2,1)} all-to-all(bf16[32,256,512]{1,0,2:T(8,128)(2,1)} %copy.79), channel_id=1, replica_groups=mesh['seq'=16,'chan'=2] {'chan'}, dimensions={2} | all-to-all | bytes 16777216 | tf_op jit(solution)/shard_map/all_to_all | solution.py:38
  982.0 7.0 all-to-all-start.2
  989.0 16.5 %copy.97 = bf16[32,256,2,256]{1,2,3,0:T(2,128)(2,1)} copy(bf16[32,256,2,256]{1,0,3,2:T(8,128)(2,1)} %bitcast.67) | data formatting | bytes 16777216 | tf_op jit(solution)/shard_map/all_to_all | solution.py:38
  1005.5 14.1 %all_to_all.54 = bf16[32,512,256]{1,2,0:T(8,128)(2,1)} reshape(bf16[32,2,256,256]{2,1,3,0:T(2,128)(2,1)} %bitcast.69) | data formatting | bytes 16777216 | tf_op jit(solution)/shard_map/all_to_all | solution.py:38
  1019.6 11.5 copy.82
  1031.1 119.3 %all-to-all-done.2 = bf16[512,256,32]{1,2,0:T(8,128)(2,1)} async-done(((bf16[512,256,32]{1,2,0:T(8,128)(2,1)}), bf16[512,256,32]{1,2,0:T(8,128)(2,1)}, u32[]{:S(2)}, u32[]{:S(2)}) %all-to-all-start.2) | async-done | bytes 8388640 | tf_op jit(solution)/shard_map/all_to_all | solution.py:46
  1150.4 16.5 %copy.98 = bf16[2,256,256,32]{2,0,1,3:T(2,128)(2,1)} copy(bf16[2,256,256,32]{2,3,1,0:T(8,128)(2,1)} %bitcast.24) | data formatting | bytes 16777216 | tf_op jit(solution)/shard_map/all_to_all | solution.py:46
  1166.9 14.0 %all_to_all.50 = bf16[256,512,32]{1,0,2:T(8,128)(2,1)} reshape(bf16[256,2,256,32]{2,1,0,3:T(2,128)(2,1)} %bitcast.70) | data formatting | bytes 16777216 | tf_op jit(solution)/shard_map/all_to_all | solution.py:46
  1181.0 15.6 %fusion.1 = bf16[32,256,512]{2,1,0:T(8,128)(2,1)} fusion(bf16[32,256,512]{2,1,0:T(8,128)(2,1)} %param.9, bf16[32,256,512]{1,2,0:T(8,128)(2,1)} %bitcast.66, bf16[32,512,512]{2,1,0:T(8,128)(2,1)} %all-gather.5.cloned.1.call-done), kind=kOutput, calls=%fused_computation.6 | convolution fusion | flops 4320133120 | bytes 41943040 | tf_op jit(solution)/shard_map/coi,cdi->cdo/dot_general | solution.py:28
  1196.6 14.0 %multiply_convert_fusion.2 = bf16[32,256,512]{2,1,0:T(8,128)(2,1)} fusion(bf16[256,512,32]{1,0,2:T(8,128)(2,1)} %all_to_all.50, bf16[512,32,512]{2,0,1:T(8,128)(2,1)} %all-gather.9.cloned.1.call-done), kind=kOutput, calls=%fused_computation.11 | convolution fusion | flops 4303355904 | bytes 33554432 | tf_op jit(solution)/shard_map/odr,dri->roi/dot_general | solution.py:48
  1210.6 13.8 %multiply_convert_fusion.1 = bf16[32,256,512]{2,1,0:T(8,128)(2,1)} fusion(bf16[32,512,256]{1,2,0:T(8,128)(2,1)} %all_to_all.54, bf16[32,512,512]{2,1,0:T(8,128)(2,1)} %all-gather.11.cloned.1.call-done), kind=kOutput, calls=%fused_computation.10 | convolution fusion | flops 4303355904 | bytes 33554432 | tf_op jit(solution)/shard_map/cdo,cdi->coi/dot_general | solution.py:40
  (42 shorter events, 48.1 us)
Async XLA Ops:
  7.2 204.0 %all-gather.5.cloned.1.call-start = ((), (), s32[]{:S(2)}) async-start(), calls=%async_computation.4 | async-start | bytes 25165824 | tf_op jit(solution)/shard_map/all_gather | solution.py:19
  7.9 403.7 %all-gather.7.cloned.1.call-start = ((), (), s32[]{:S(2)}) async-start(), calls=%async_computation.5 | async-start | bytes 25165824 | tf_op jit(solution)/shard_map/all_gather | solution.py:18
  239.3 9.4 copy-start.2
  250.2 20.7 %copy-start.1 = (bf16[1,32,256,32]{3,2,1,0:T(8,128)(2,1)S(1)}, bf16[1,32,256,32]{3,2,1,0:T(8,128)(2,1)}, u32[]{:S(2)}) copy-start(bf16[1,32,256,32]{3,2,1,0:T(8,128)(2,1)} %get-tuple-element.22) | copy-start | bytes 1572868
  271.7 14.9 %copy-start = (bf16[1,32,256,32]{3,2,1,0:T(8,128)(2,1)S(1)}, bf16[1,32,256,32]{3,2,1,0:T(8,128)(2,1)}, u32[]{:S(2)}) copy-start(bf16[1,32,256,32]{3,2,1,0:T(8,128)(2,1)} %get-tuple-element.29) | copy-start | bytes 1572868
  301.0 156.4 %all-to-all-start = ((bf16[16,32,256,32]{2,3,1,0:T(8,128)(2,1)}), bf16[16,32,256,32]{2,3,1,0:T(8,128)(2,1)}, u32[]{:S(2)}, u32[]{:S(2)}) async-start(bf16[16,32,256,32]{2,3,1,0:T(8,128)(2,1)} %constant_dynamic-update-slice_fusion), calls=%async_computation | async-start | bytes 16777216 | tf_op jit(solution)/shard_map/all_to_all | solution.py:44
  306.8 889.9 %all-gather.9.cloned.1.call-start = ((), (), s32[]{:S(2)}) async-start(), calls=%async_computation.6 | async-start | bytes 25165824 | tf_op jit(solution)/shard_map/all_gather | solution.py:16
  501.4 709.3 %all-gather.11.cloned.1.call-start = ((), (), s32[]{:S(2)}) async-start(), calls=%async_computation.7 | async-start | bytes 25165824 | tf_op jit(solution)/shard_map/all_gather | solution.py:26
  982.0 168.4 %all-to-all-start.2 = ((bf16[512,256,32]{1,2,0:T(8,128)(2,1)}), bf16[512,256,32]{1,2,0:T(8,128)(2,1)}, u32[]{:S(2)}, u32[]{:S(2)}) async-start(bf16[512,256,32]{1,2,0:T(8,128)(2,1)} %bitcast.23), calls=%async_computation.2 | async-start | bytes 16777216 | tf_op jit(solution)/shard_map/all_to_all | solution.py:46
Sparse Core Ops, SparseCore 0:
  9.5 201.5 all-gather.4
  212.7 198.8 all-gather.6
  501.5 229.9 all-gather.8
  771.8 357.3 all-gather.10
